TPU v7x, 512 devices: a whole 4x8x8 slice. The times are simulated.
512 devices in a mesh: wide: 32 (over y, z_hi, core), grp: 16 (over x, z_lo).
Axes of the slice: x: 4, y: 8, z: 8 (z_hi: 2, z_lo: 4; z = z_hi * 4 + z_lo), core: 2. Of those that a mesh axis runs over, the one named last changes fastest.
Arguments:
- obs_value: float32 [65536], P(('wide', 'grp')), may hold values from -6 to 6
- obs_tile: int32 [65536], P(('wide', 'grp')), may hold values from 0 to 31
- obs_cell: int32 [65536], P(('wide', 'grp')), may hold values from 0 to 32767
- obs_type: int32 [65536], P(('wide', 'grp')), may hold values from 0 to 2
- obs_weights: float32 [2, 8], replicated, may hold values from 0.2 to 1.5
- diffusivity: float32 [128, 8192], P('wide', 'grp'), may hold values from 0.03 to 0.24
- erodibility: float32 [128, 8192], P('wide', 'grp'), may hold values from 0.1 to 1
- class_mixing: float32 [8, 8], replicated, may hold values from -2.5 to 2.5
- fall_table: float32 [16], replicated, may hold values from 0.05 to 0.6
- fall_index: int32 [8], replicated, may hold values from 0 to 15
- bedload_rate: float32 [8], replicated, may hold values from 20 to 3000
Outputs:
- adjoint_tracer: float32 [8, 16, 128, 8192], P(None, None, 'wide', 'grp')
- adjoint_bed: float32 [8, 128, 8192], P(None, 'wide', 'grp')
All inputs are finite; a program needn't handle non-finite values.
Results may differ from a plain program's by a relative error of at most 0.00019.
Values sent between devices are 32-bit elements; how exact they have to be, the bound alone decides.
No kernel may reach another device: no remote copies, remote signals or barrier semaphores. Data moves between devices by JAX's collectives and lax.ppermute only.
A program may use at most 64 MiB of HBM per device.

v0:
```python
import jax
import jax.numpy as jnp
from jax import lax
from jax.sharding import PartitionSpec as P

K = 16
STEPS = 2


def padded_2(array, sides, width):
    for axis, dim in sides:
        peers, length = (lax.axis_size(axis), array.shape[dim])
        up = [(i, (i + 1) % peers) for i in range(peers - 1)]
        down = [(j, i) for i, j in up]
        last = lax.slice_in_dim(array, length - width, length, axis=dim)
        first = lax.slice_in_dim(array, 0, width, axis=dim)
        before = lax.ppermute(last, axis, up)
        after = lax.ppermute(first, axis, down)
        array = jnp.concatenate([before, array, after], axis=dim)
    return array


def link(earlier, later):
    return (earlier[0] * later[0], later[0] * earlier[1] + later[1])


def local_sweep(rows, rate_rows):
    gain_f = 1.0 / (1.0 + rate_rows)
    gain_g = rate_rows / (1.0 + rate_rows)
    flipped = rows[:, ::-1]
    coeff = jnp.broadcast_to(gain_g[:, None], flipped.shape)
    return lax.associative_scan(link, (coeff, gain_f[:, None] * flipped), axis=1)


def local(
    obs_value,
    obs_tile,
    obs_cell,
    obs_type,
    obs_weights,
    diffusivity,
    erodibility,
    class_mixing,
    fall_table,
    fall_index,
    bedload_rate,
):
    classes = obs_weights.shape[1]
    tile_x, tile_y = diffusivity.shape
    cells = K * tile_x * tile_y
    values, tiles, places, kinds = (
        lax.all_gather(obs_value, "wide", axis=0, tiled=True),
        lax.all_gather(obs_tile, "wide", axis=0, tiled=True),
        lax.all_gather(obs_cell, "wide", axis=0, tiled=True),
        lax.all_gather(obs_type, "wide", axis=0, tiled=True),
    )
    mine = jnp.logical_and(kinds < 2, tiles == lax.axis_index("wide"))
    live = jnp.where(mine, values, 0.0)
    kind = jnp.where(kinds < 2, kinds, 0)
    fields = jnp.zeros((2, cells), jnp.float32).at[kind, places].add(live)
    fields = fields.reshape(2, K, tile_x, tile_y)
    lq = jnp.einsum("tc,tkxy->ckxy", obs_weights, fields, precision=lax.Precision.HIGHEST)
    lb = jnp.zeros((classes, tile_x, tile_y), jnp.float32)
    table_hit = fall_index[:, None] == jnp.arange(fall_table.shape[0], dtype=jnp.int32)[None, :]
    settle = jnp.sum(jnp.where(table_hit, fall_table[None, :], 0.0), axis=1)
    rate_rows = jnp.repeat(bedload_rate, tile_x)
    for step in range(STEPS):
        lb = lb + erodibility * jnp.einsum(
            "cd,cxy->dxy", class_mixing, lq[:, 0], precision=lax.Precision.HIGHEST
        )
        rows = lb.reshape(classes * tile_x, tile_y)
        moved = lax.all_to_all(rows, "grp", split_axis=0, concat_axis=1, tiled=True)
        share = moved.shape[0]
        my_rates = lax.dynamic_slice_in_dim(rate_rows, lax.axis_index("grp") * share, share)
        swept = local_sweep(moved, my_rates)
        solved = swept[1][:, ::-1]
        rows = lax.all_to_all(solved, "grp", split_axis=1, concat_axis=0, tiled=True)
        lb = rows.reshape(classes, tile_x, tile_y)
        lq = lq.at[:, 0].add(settle[:, None, None] * lb)
        below = jnp.concatenate([jnp.zeros_like(lq[:, :1]), lq[:, :-1]], axis=1)
        lq = (1.0 - settle)[:, None, None, None] * lq + settle[:, None, None, None] * below
        moment = diffusivity * lq
        padded = padded_2(moment, (("wide", 2), ("grp", 3)), 1)
        beside = (
            padded[:, :, 2:, 1:-1]
            + padded[:, :, :-2, 1:-1]
            + padded[:, :, 1:-1, 2:]
            + padded[:, :, 1:-1, :-2]
        )
        lq = lq - 4.0 * moment + beside
    return (lq, lb)


def solution(mesh):
    in_specs = (
        P(("wide", "grp")),
        P(("wide", "grp")),
        P(("wide", "grp")),
        P(("wide", "grp")),
        P(),
        P("wide", "grp"),
        P("wide", "grp"),
        P(),
        P(),
        P(),
        P(),
    )
    out_specs = (P(None, None, "wide", "grp"), P(None, "wide", "grp"))
    return jax.shard_map(local, mesh=mesh, in_specs=in_specs, out_specs=out_specs, check_vma=False)
```

profile of v0, /device:TPU:5, one launch (start us, length us, event | category | flops | bytes accessed | tf_op | source)
XLA Modules:
  0.0 467.2 jit_solution(3767252619659113177)
XLA Ops:
  1.3 58.4 %all-gather.3 = f32[32,1,128]{2,1,0:T(1,128)S(1)} all-gather(f32[1,1,128]{2,1,0:T(1,128)S(1)} %bitcast.94), channel_id=1, replica_groups=mesh['wide'=32,'grp'=16] {'wide'}, dimensions={0}, use_global_device_ids=true | all-gather | bytes 16896 | tf_op jit(solution)/shard_map/all_gather | solution.py:52
  60.4 46.3 %all-gather.2 = s32[32,1,128]{2,1,0:T(1,128)S(1)} all-gather(s32[1,1,128]{2,1,0:T(1,128)S(1)} %bitcast.95), channel_id=1, replica_groups=mesh['wide'=32,'grp'=16] {'wide'}, dimensions={0}, use_global_device_ids=true | all-gather | bytes 16896 | tf_op jit(solution)/shard_map/all_gather | solution.py:53
  107.4 51.6 %all-gather.1 = s32[32,1,128]{2,1,0:T(1,128)S(1)} all-gather(s32[1,1,128]{2,1,0:T(1,128)S(1)} %bitcast.96), channel_id=1, replica_groups=mesh['wide'=32,'grp'=16] {'wide'}, dimensions={0}, use_global_device_ids=true | all-gather | bytes 16896 | tf_op jit(solution)/shard_map/all_gather | solution.py:54
  159.6 46.3 %all-gather = s32[32,1,128]{2,1,0:T(1,128)S(1)} all-gather(s32[1,1,128]{2,1,0:T(1,128)S(1)} %bitcast.97), channel_id=1, replica_groups=mesh['wide'=32,'grp'=16] {'wide'}, dimensions={0}, use_global_device_ids=true | all-gather | bytes 16896 | tf_op jit(solution)/shard_map/all_gather | solution.py:55
  207.4 22.0 %scatter_custom_fusion = f32[65536]{0:T(1024)S(1)} fusion(s32[4096]{0:T(1024)S(1)} %broadcast_select_fusion, f32[4096]{0:T(1024)S(1)} %fusion.25, f32[]{:T(128)} %constant.65.clone.1), kind=kCustom, calls=%fused_computation.42 | custom fusion | flops 4096 | bytes 262148
  230.1 1.2 fusion.11
  232.3 7.0 %all-to-all-start = ((f32[16,2,512]{2,1,0:T(2,128)}), f32[16,2,512]{2,1,0:T(2,128)S(1)}, u32[]{:S(2)}, u32[]{:S(2)}) async-start(f32[16,2,512]{2,1,0:T(2,128)} %all_to_all.52), calls=%async_computation | async-start | bytes 131072 | tf_op jit(solution)/shard_map/all_to_all | solution.py:72
  241.3 3.3 all-to-all-done
  244.6 5.6 %rev.12 = f32[2,8192]{1,0:T(2,128)S(1)} reverse(f32[2,8192]{1,0:T(2,128)S(1)} %bitcast.71), dimensions={1} | reverse | bytes 131072 | tf_op jit(solution)/shard_map/rev | solution.py:30
  250.3 1.4 slice.706
  251.8 1.3 slice.626
  253.1 1.5 slice.625
  271.4 0.9 pad.186
  273.9 1.6 pad.188
  275.6 1.8 pad.189
  277.5 20.6 %rev.13 = f32[2,8192]{1,0:T(2,128)} reverse(f32[2,8192]{1,0:T(2,128)S(1)} %add.446), dimensions={1} | reverse | bytes 131072 | tf_op jit(solution)/shard_map/rev | solution.py:76
  298.1 5.0 %all-to-all-start.1 = ((f32[2,16,512]{2,0,1:T(2,128)}), f32[2,16,512]{2,0,1:T(2,128)S(1)}, u32[]{:S(2)}, u32[]{:S(2)}) async-start(f32[2,16,512]{2,0,1:T(2,128)} %bitcast.22), calls=%async_computation.1 | async-start | bytes 131072 | tf_op jit(solution)/shard_map/all_to_all | solution.py:77
  303.2 5.1 %all-to-all-done.1 = f32[2,16,512]{2,0,1:T(2,128)S(1)} async-done(((f32[2,16,512]{2,0,1:T(2,128)}), f32[2,16,512]{2,0,1:T(2,128)S(1)}, u32[]{:S(2)}, u32[]{:S(2)}) %all-to-all-start.1) | async-done | bytes 65568 | tf_op jit(solution)/shard_map/all_to_all | solution.py:77
  310.1 9.9 %collective-permute-start.1 = (f32[8,16,1,512]{3,0,2,1:T(8,128)S(1)}, f32[8,16,1,512]{3,0,2,1:T(8,128)S(1)}, u32[]{:S(2)}, u32[]{:S(2)}) collective-permute-start(f32[8,16,1,512]{3,0,2,1:T(8,128)S(1)} %get-tuple-element.47), channel_id=1, source_target_pairs={{0,16},{16,32},{32,48},{48,64},{64,80},{80,96},{96,112},{112,128},... | collective-permute-start | bytes 786440 | tf_op jit(solution)/shard_map/ppermute | solution.py:17
  320.0 1.9 collective-permute-start
  321.9 10.1 %collective-permute-done.1 = f32[8,16,1,512]{3,0,2,1:T(8,128)S(1)} collective-permute-done((f32[8,16,1,512]{3,0,2,1:T(8,128)S(1)}, f32[8,16,1,512]{3,0,2,1:T(8,128)S(1)}, u32[]{:S(2)}, u32[]{:S(2)}) %collective-permute-start.1) | collective-permute-done | bytes 262176 | tf_op jit(solution)/shard_map/ppermute | solution.py:17
  331.9 1.4 collective-permute-done
  333.3 0.9 pad_maximum_fusion.21
  334.2 3.5 collective-permute-start.2
  337.7 1.9 collective-permute-start.3
  339.7 9.3 %collective-permute-done.2 = f32[8,16,6,1]{3,0,2,1:T(8,128)S(1)} collective-permute-done((f32[8,16,6,1]{3,0,2,1:T(8,128)}, f32[8,16,6,1]{3,0,2,1:T(8,128)S(1)}, u32[]{:S(2)}, u32[]{:S(2)}) %collective-permute-start.2) | collective-permute-done | bytes 3104 | tf_op jit(solution)/shard_map/ppermute | solution.py:18
  349.8 2.3 fusion.8
  352.5 10.3 %all_to_all.70 = f32[16,2,512]{2,1,0:T(2,128)S(1)} all-to-all(f32[16,2,512]{2,1,0:T(2,128)S(1)} %all_to_all.59), channel_id=1, replica_groups=mesh['wide'=32,'grp'=16] {'grp'}, dimensions={0} | all-to-all | bytes 131072 | tf_op jit(solution)/shard_map/all_to_all | solution.py:72
  362.8 5.6 %rev.14 = f32[2,8192]{1,0:T(2,128)S(1)} reverse(f32[2,8192]{1,0:T(2,128)S(1)} %bitcast.72), dimensions={1} | reverse | bytes 131072 | tf_op jit(solution)/shard_map/rev | solution.py:30
  368.4 1.4 slice.778
  369.9 1.3 slice.719
  371.2 1.3 slice.718
  395.4 0.9 pad.212
  398.0 1.6 pad.214
  399.6 1.9 pad.215
  401.6 5.6 %rev.15 = f32[2,8192]{1,0:T(2,128)S(1)} reverse(f32[2,8192]{1,0:T(2,128)S(1)} %add.491), dimensions={1} | reverse | bytes 131072 | tf_op jit(solution)/shard_map/rev | solution.py:76
  407.1 9.6 %all_to_all.71 = f32[2,16,512]{2,0,1:T(2,128)S(1)} all-to-all(f32[2,16,512]{2,0,1:T(2,128)S(1)} %bitcast.73), channel_id=1, replica_groups=mesh['wide'=32,'grp'=16] {'grp'}, dimensions={1} | all-to-all | bytes 131072 | tf_op jit(solution)/shard_map/all_to_all | solution.py:77
  418.4 13.4 %collective-permute-start.5 = (f32[8,16,1,512]{3,0,2,1:T(8,128)S(1)}, f32[8,16,1,512]{3,0,2,1:T(8,128)S(1)}, u32[]{:S(2)}, u32[]{:S(2)}) collective-permute-start(f32[8,16,1,512]{3,0,2,1:T(8,128)S(1)} %get-tuple-element.45), channel_id=1, source_target_pairs={{0,16},{16,32},{32,48},{48,64},{64,80},{80,96},{96,112},{112,128},... | collective-permute-start | bytes 786440 | tf_op jit(solution)/shard_map/ppermute | solution.py:17
  431.7 1.9 collective-permute-start.4
  433.7 7.6 %collective-permute-done.5 = f32[8,16,1,512]{3,0,2,1:T(8,128)S(1)} collective-permute-done((f32[8,16,1,512]{3,0,2,1:T(8,128)S(1)}, f32[8,16,1,512]{3,0,2,1:T(8,128)S(1)}, u32[]{:S(2)}, u32[]{:S(2)}) %collective-permute-start.5) | collective-permute-done | bytes 262176 | tf_op jit(solution)/shard_map/ppermute | solution.py:17
  441.3 2.2 collective-permute-done.4
  443.5 1.0 pad_maximum_fusion.18
  444.5 4.1 collective-permute-start.6
  448.6 2.5 collective-permute-start.7
  451.8 4.8 %collective-permute-done.6 = f32[8,16,6,1]{3,0,2,1:T(8,128)} collective-permute-done((f32[8,16,6,1]{3,0,2,1:T(8,128)}, f32[8,16,6,1]{3,0,2,1:T(8,128)}, u32[]{:S(2)}, u32[]{:S(2)}) %collective-permute-start.6) | collective-permute-done | bytes 3104 | tf_op jit(solution)/shard_map/ppermute | solution.py:18
  456.6 6.6 %collective-permute-done.7 = f32[8,16,6,1]{3,0,2,1:T(8,128)} collective-permute-done((f32[8,16,6,1]{3,0,2,1:T(8,128)}, f32[8,16,6,1]{3,0,2,1:T(8,128)}, u32[]{:S(2)}, u32[]{:S(2)}) %collective-permute-start.7) | collective-permute-done | bytes 3104 | tf_op jit(solution)/shard_map/ppermute | solution.py:17
  463.2 1.9 fusion.4
  465.1 1.6 copy.75
  (392 shorter events, 55.6 us)
Async XLA Ops:
  0.6 230.6 %copy-start = (f32[8,8]{1,0:T(8,128)S(1)}, f32[8,8]{1,0:T(8,128)}, u32[]{:S(2)}) copy-start(f32[8,8]{1,0:T(8,128)} %param.22) | copy-start | bytes 772
  229.4 0.7 copy-start.52
  230.1 1.2 copy-start.14
  232.3 12.4 %all-to-all-start = ((f32[16,2,512]{2,1,0:T(2,128)}), f32[16,2,512]{2,1,0:T(2,128)S(1)}, u32[]{:S(2)}, u32[]{:S(2)}) async-start(f32[16,2,512]{2,1,0:T(2,128)} %all_to_all.52), calls=%async_computation | async-start | bytes 131072 | tf_op jit(solution)/shard_map/all_to_all | solution.py:72
  240.2 10.1 %copy-start.44 = (f32[2]{0:T(128)}, f32[2]{0:T(128)S(1)}, u32[]{:S(2)}) copy-start(f32[2]{0:T(128)S(1)} %get-tuple-element.65) | copy-start | bytes 28
  240.2 22.6 %copy-start.46 = (f32[2]{0:T(128)}, f32[2]{0:T(128)S(1)}, u32[]{:S(2)}) copy-start(f32[2]{0:T(128)S(1)} %get-tuple-element.37) | copy-start | bytes 28
  240.2 24.3 %copy-start.22 = (f32[2]{0:T(128)}, f32[2]{0:T(128)S(1)}, u32[]{:S(2)}) copy-start(f32[2]{0:T(128)S(1)} %get-tuple-element.38) | copy-start | bytes 28
  240.2 27.5 %copy-start.20 = (f32[2]{0:T(128)}, f32[2]{0:T(128)S(1)}, u32[]{:S(2)}) copy-start(f32[2]{0:T(128)S(1)} %get-tuple-element.39) | copy-start | bytes 28
  240.2 24.7 %copy-start.32 = (f32[2]{0:T(128)}, f32[2]{0:T(128)S(1)}, u32[]{:S(2)}) copy-start(f32[2]{0:T(128)S(1)} %get-tuple-element.68) | copy-start | bytes 28
  240.2 25.2 %copy-start.30 = (f32[2]{0:T(128)}, f32[2]{0:T(128)S(1)}, u32[]{:S(2)}) copy-start(f32[2]{0:T(128)S(1)} %get-tuple-element.66) | copy-start | bytes 28
  240.2 26.2 %copy-start.40 = (f32[2]{0:T(128)}, f32[2]{0:T(128)S(1)}, u32[]{:S(2)}) copy-start(f32[2]{0:T(128)S(1)} %get-tuple-element.67) | copy-start | bytes 28
  240.2 28.7 %copy-start.28 = (f32[2]{0:T(128)}, f32[2]{0:T(128)S(1)}, u32[]{:S(2)}) copy-start(f32[2]{0:T(128)S(1)} %get-tuple-element.61) | copy-start | bytes 28
  240.2 30.4 %copy-start.26 = (f32[2]{0:T(128)}, f32[2]{0:T(128)S(1)}, u32[]{:S(2)}) copy-start(f32[2]{0:T(128)S(1)} %get-tuple-element.62) | copy-start | bytes 28
  240.3 23.1 %copy-start.38 = (f32[2]{0:T(128)}, f32[2]{0:T(128)S(1)}, u32[]{:S(2)}) copy-start(f32[2]{0:T(128)S(1)} %get-tuple-element.57) | copy-start | bytes 28
  240.3 23.5 %copy-start.36 = (f32[2]{0:T(128)}, f32[2]{0:T(128)S(1)}, u32[]{:S(2)}) copy-start(f32[2]{0:T(128)S(1)} %get-tuple-element.63) | copy-start | bytes 28
  240.3 23.8 %copy-start.34 = (f32[2]{0:T(128)}, f32[2]{0:T(128)S(1)}, u32[]{:S(2)}) copy-start(f32[2]{0:T(128)S(1)} %get-tuple-element.58) | copy-start | bytes 28
  240.5 22.3 %copy-start.48 = (f32[2,1]{1,0:T(2,128)}, f32[2,1]{1,0:T(2,128)S(1)}, u32[]{:S(2)}) copy-start(f32[2,1]{1,0:T(2,128)S(1)} %copy.64) | copy-start | bytes 28
  241.2 21.9 %copy-start.50 = (f32[2,1]{1,0:T(2,128)}, f32[2,1]{1,0:T(2,128)S(1)}, u32[]{:S(2)}) copy-start(f32[2,1]{1,0:T(2,128)S(1)} %copy.65) | copy-start | bytes 28
  241.3 67.2 %copy-start.24 = (f32[8]{0:T(128)}, f32[8]{0:T(128)S(1)}, u32[]{:S(2)}) copy-start(f32[8]{0:T(128)S(1)} %select_reduce_fusion) | copy-start | bytes 100
  250.3 2.8 copy-start.5
  254.7 1.3 copy-start.7
  256.7 0.7 copy-start.9
  265.4 0.7 slice-start.10
  270.7 0.7 slice-start.2
  273.2 0.7 slice-start.1
  298.1 10.2 %all-to-all-start.1 = ((f32[2,16,512]{2,0,1:T(2,128)}), f32[2,16,512]{2,0,1:T(2,128)S(1)}, u32[]{:S(2)}, u32[]{:S(2)}) async-start(f32[2,16,512]{2,0,1:T(2,128)} %bitcast.22), calls=%async_computation.1 | async-start | bytes 131072 | tf_op jit(solution)/shard_map/all_to_all | solution.py:77
  303.1 5.4 %copy-start.42 = (f32[8]{0:T(128)}, f32[8]{0:T(128)S(1)}, u32[]{:S(2)}) copy-start(f32[8]{0:T(128)S(1)} %broadcast_subtract_fusion) | copy-start | bytes 100
  308.4 0.7 copy-start.13
  309.1 0.9 copy-start.1
  310.1 21.8 %collective-permute-start.1 = (f32[8,16,1,512]{3,0,2,1:T(8,128)S(1)}, f32[8,16,1,512]{3,0,2,1:T(8,128)S(1)}, u32[]{:S(2)}, u32[]{:S(2)}) collective-permute-start(f32[8,16,1,512]{3,0,2,1:T(8,128)S(1)} %get-tuple-element.47), channel_id=1, source_target_pairs={{0,16},{16,32},{32,48},{48,64},{64,80},{80,96},{96,112},{112,128},... | collective-permute-start | bytes 786440 | tf_op jit(solution)/shard_map/ppermute | solution.py:17
  320.0 13.3 %collective-permute-start = (f32[8,16,1,512]{3,0,2,1:T(8,128)S(1)}, f32[8,16,1,512]{3,0,2,1:T(8,128)S(1)}, u32[]{:S(2)}, u32[]{:S(2)}) collective-permute-start(f32[8,16,1,512]{3,0,2,1:T(8,128)S(1)} %get-tuple-element.48), channel_id=1, source_target_pairs={{16,0},{32,16},{48,32},{64,48},{80,64},{96,80},{112,96},{128,112},... | collective-permute-start | bytes 786440 | tf_op jit(solution)/shard_map/ppermute | solution.py:18
  333.3 0.9 copy-start.3
  334.2 14.8 %collective-permute-start.2 = (f32[8,16,6,1]{3,0,2,1:T(8,128)}, f32[8,16,6,1]{3,0,2,1:T(8,128)S(1)}, u32[]{:S(2)}, u32[]{:S(2)}) collective-permute-start(f32[8,16,6,1]{3,0,2,1:T(8,128)} %get-tuple-element.43), channel_id=1, source_target_pairs={{1,0},{2,1},{3,2},{4,3},{5,4},{6,5},{7,6},{8,7},{9,8},{10,9},{11,1... | collective-permute-start | bytes 9224 | tf_op jit(solution)/shard_map/ppermute | solution.py:18
  337.7 12.1 %collective-permute-start.3 = (f32[8,16,6,1]{3,0,2,1:T(8,128)S(1)}, f32[8,16,6,1]{3,0,2,1:T(8,128)}, u32[]{:S(2)}, u32[]{:S(2)}) collective-permute-start(f32[8,16,6,1]{3,0,2,1:T(8,128)S(1)} %get-tuple-element.44), channel_id=1, source_target_pairs={{0,1},{1,2},{2,3},{3,4},{4,5},{5,6},{6,7},{7,8},{8,9},{9,10},{10,1... | collective-permute-start | bytes 9224 | tf_op jit(solution)/shard_map/ppermute | solution.py:17
  339.7 12.4 %copy-start.15 = (f32[4,512]{1,0:T(4,128)S(1)}, f32[4,512]{1,0:T(4,128)}, u32[]{:S(2)}) copy-start(f32[4,512]{1,0:T(4,128)} %param.21) | copy-start | bytes 24580
  349.0 0.8 copy-start.6
  362.8 5.6 %copy-start.45 = (f32[2]{0:T(128)S(1)}, f32[2]{0:T(128)}, u32[]{:S(2)}) copy-start(f32[2]{0:T(128)} %copy-done.44) | copy-start | bytes 28
  368.4 2.8 copy-start.4
  372.6 1.3 copy-start.8
  374.7 0.7 copy-start.10
  381.4 0.7 copy-start.23
  383.2 0.7 copy-start.37
  389.5 0.7 slice-start.11
  418.4 22.9 %collective-permute-start.5 = (f32[8,16,1,512]{3,0,2,1:T(8,128)S(1)}, f32[8,16,1,512]{3,0,2,1:T(8,128)S(1)}, u32[]{:S(2)}, u32[]{:S(2)}) collective-permute-start(f32[8,16,1,512]{3,0,2,1:T(8,128)S(1)} %get-tuple-element.45), channel_id=1, source_target_pairs={{0,16},{16,32},{32,48},{48,64},{64,80},{80,96},{96,112},{112,128},... | collective-permute-start | bytes 786440 | tf_op jit(solution)/shard_map/ppermute | solution.py:17
  431.7 11.7 %collective-permute-start.4 = (f32[8,16,1,512]{3,0,2,1:T(8,128)S(1)}, f32[8,16,1,512]{3,0,2,1:T(8,128)S(1)}, u32[]{:S(2)}, u32[]{:S(2)}) collective-permute-start(f32[8,16,1,512]{3,0,2,1:T(8,128)S(1)} %get-tuple-element.46), channel_id=1, source_target_pairs={{16,0},{32,16},{48,32},{64,48},{80,64},{96,80},{112,96},{128,112},... | collective-permute-start | bytes 786440 | tf_op jit(solution)/shard_map/ppermute | solution.py:18
  443.5 1.0 copy-start.2
  444.5 12.1 %collective-permute-start.6 = (f32[8,16,6,1]{3,0,2,1:T(8,128)}, f32[8,16,6,1]{3,0,2,1:T(8,128)}, u32[]{:S(2)}, u32[]{:S(2)}) collective-permute-start(f32[8,16,6,1]{3,0,2,1:T(8,128)} %get-tuple-element.41), channel_id=1, source_target_pairs={{1,0},{2,1},{3,2},{4,3},{5,4},{6,5},{7,6},{8,7},{9,8},{10,9},{11,1... | collective-permute-start | bytes 9224 | tf_op jit(solution)/shard_map/ppermute | solution.py:18
  448.6 14.6 %collective-permute-start.7 = (f32[8,16,6,1]{3,0,2,1:T(8,128)}, f32[8,16,6,1]{3,0,2,1:T(8,128)}, u32[]{:S(2)}, u32[]{:S(2)}) collective-permute-start(f32[8,16,6,1]{3,0,2,1:T(8,128)} %get-tuple-element.42), channel_id=1, source_target_pairs={{0,1},{1,2},{2,3},{3,4},{4,5},{5,6},{6,7},{7,8},{8,9},{9,10},{10,1... | collective-permute-start | bytes 9224 | tf_op jit(solution)/shard_map/ppermute | solution.py:17
  (36 other events, 23.4 us)
where the time goes:
time: 474 us; the launch traced here: 467 us
  blocking collectives  223 us (47%)
  local copies, waits for them, and re-layouts  104 us (22%)
  starting transfers between devices  51.1 us (11%)
  waiting for transfers between devices  50.3 us (11%)
  other arithmetic  35.5 us (7%)
    all_gather x1, blocking collectives, local(): lax.all_gather(obs_value, 'wide', axis=0, tiled=True)  58.4 us
    all_gather x1, blocking collectives, local(): lax.all_gather(obs_cell, 'wide', axis=0, tiled=True)  51.6 us
    all_gather x1, blocking collectives, local(): lax.all_gather(obs_tile, 'wide', axis=0, tiled=True)  46.3 us
    all_gather x1, blocking collectives, local(): lax.all_gather(obs_type, 'wide', axis=0, tiled=True)  46.3 us
    slice x94, local copies, waits for them, and re-layouts, local_sweep(): lax.associative_scan(link, (coeff, gain_f[:, None] * flipped), axis=1)  29.3 us
    ppermute x4, starting transfers between devices, padded_2(): before = lax.ppermute(last, axis, up)  27.6 us
    rev x2, local copies, waits for them, and re-layouts, local(): solved = swept[1][:, ::-1]  26.2 us
    ppermute x4, waiting for transfers between devices, padded_2(): before = lax.ppermute(last, axis, up)  24.3 us
  transfers between devices with their start and end apart: 10, of which 9 were waited for; matrix products, arithmetic and copies ran while one was open for 0% of the time, Pallas kernels for 0%

commit v1 on v0

--- a/solution.py
+++ b/solution.py
@@ -5,6 +5,12 @@
 
 K = 16
 STEPS = 2
+
+
+def boxes_match(axis_tag, load):
+    current_arr = jnp.stack([load] * lax.axis_size(axis_tag), 0)
+    low = lax.all_to_all(current_arr, axis_tag, 0, 0)
+    return jnp.concatenate(low, 0)
 
 
 def padded_2(array, sides, width):
@@ -49,7 +55,7 @@
     tile_x, tile_y = diffusivity.shape
     cells = K * tile_x * tile_y
     values, tiles, places, kinds = (
-        lax.all_gather(obs_value, "wide", axis=0, tiled=True),
+        boxes_match("wide", obs_value),
         lax.all_gather(obs_tile, "wide", axis=0, tiled=True),
         lax.all_gather(obs_cell, "wide", axis=0, tiled=True),
         lax.all_gather(obs_type, "wide", axis=0, tiled=True),

time: 474 us -> 442 us (0.932)
  the two profiles are of different devices: /device:TPU:5 before, /device:TPU:35 now
where the time goes in v1:
time: 442 us; the launch traced here: 435 us
  blocking collectives  170 us (38%)
  local copies, waits for them, and re-layouts  104 us (24%)
  waiting for transfers between devices  62.3 us (14%)
  starting transfers between devices  59.2 us (13%)
  other arithmetic  35.5 us (8%)
    all_gather x1, blocking collectives, local(): lax.all_gather(obs_cell, 'wide', axis=0, tiled=True)  51.6 us
    all_gather x1, blocking collectives, local(): lax.all_gather(obs_tile, 'wide', axis=0, tiled=True)  51.4 us
    all_gather x1, blocking collectives, local(): lax.all_gather(obs_type, 'wide', axis=0, tiled=True)  46.6 us
    slice x94, local copies, waits for them, and re-layouts, local_sweep(): lax.associative_scan(link, (coeff, gain_f[:, None] * flipped), axis=1)  29.3 us
    ppermute x4, waiting for transfers between devices, padded_2(): after = lax.ppermute(first, axis, down)  29.1 us
    rev x2, local copies, waits for them, and re-layouts, local(): solved = swept[1][:, ::-1]  26.2 us
    ppermute x4, waiting for transfers between devices, padded_2(): before = lax.ppermute(last, axis, up)  22.3 us
    unnamed x4, other arithmetic  22.2 us
  transfers between devices with their start and end apart: 11, of which 10 were waited for; matrix products, arithmetic and copies ran while one was open for 0% of the time, Pallas kernels for 0%

profile of v1, /device:TPU:35, one launch (start us, length us, event | category | flops | bytes accessed | tf_op | source)
XLA Modules:
  0.0 435.3 jit_solution(8111914809673998528)
XLA Ops:
  0.6 1.3 stack.2
  1.9 16.1 %all-to-all-start = ((f32[32,1,128]{2,1,0:T(1,128)}), f32[32,1,128]{2,1,0:T(1,128)S(1)}, u32[]{:S(2)}, u32[]{:S(2)}) async-start(f32[32,1,128]{2,1,0:T(1,128)} %stack.2), calls=%async_computation | async-start | bytes 32768 | tf_op jit(solution)/shard_map/all_to_all | solution.py:12
  19.5 51.6 %all-gather.1 = s32[32,1,128]{2,1,0:T(1,128)S(1)} all-gather(s32[1,1,128]{2,1,0:T(1,128)S(1)} %bitcast.93), channel_id=1, replica_groups=mesh['wide'=32,'grp'=16] {'wide'}, dimensions={0}, use_global_device_ids=true | all-gather | bytes 16896 | tf_op jit(solution)/shard_map/all_gather | solution.py:60
  71.8 46.6 %all-gather = s32[32,1,128]{2,1,0:T(1,128)S(1)} all-gather(s32[1,1,128]{2,1,0:T(1,128)S(1)} %bitcast.94), channel_id=1, replica_groups=mesh['wide'=32,'grp'=16] {'wide'}, dimensions={0}, use_global_device_ids=true | all-gather | bytes 16896 | tf_op jit(solution)/shard_map/all_gather | solution.py:61
  120.6 51.4 %all-gather.2 = s32[32,1,128]{2,1,0:T(1,128)S(1)} all-gather(s32[1,1,128]{2,1,0:T(1,128)S(1)} %bitcast.95), channel_id=1, replica_groups=mesh['wide'=32,'grp'=16] {'wide'}, dimensions={0}, use_global_device_ids=true | all-gather | bytes 16896 | tf_op jit(solution)/shard_map/all_gather | solution.py:59
  172.0 22.0 %scatter_custom_fusion = f32[65536]{0:T(1024)S(1)} fusion(s32[4096]{0:T(1024)S(1)} %broadcast_select_fusion, f32[4096]{0:T(1024)S(1)} %fusion.25, f32[]{:T(128)} %constant.65.clone.1), kind=kCustom, calls=%fused_computation.42 | custom fusion | flops 4096 | bytes 262148
  194.7 1.2 fusion.11
  196.8 7.0 %all-to-all-start.1 = ((f32[16,2,512]{2,1,0:T(2,128)}), f32[16,2,512]{2,1,0:T(2,128)S(1)}, u32[]{:S(2)}, u32[]{:S(2)}) async-start(f32[16,2,512]{2,1,0:T(2,128)} %all_to_all.57), calls=%async_computation.1 | async-start | bytes 131072 | tf_op jit(solution)/shard_map/all_to_all | solution.py:78
  204.9 4.9 %all-to-all-done.1 = f32[16,2,512]{2,1,0:T(2,128)S(1)} async-done(((f32[16,2,512]{2,1,0:T(2,128)}), f32[16,2,512]{2,1,0:T(2,128)S(1)}, u32[]{:S(2)}, u32[]{:S(2)}) %all-to-all-start.1) | async-done | bytes 65568 | tf_op jit(solution)/shard_map/all_to_all | solution.py:78
  209.8 5.6 %rev.12 = f32[2,8192]{1,0:T(2,128)S(1)} reverse(f32[2,8192]{1,0:T(2,128)S(1)} %bitcast.70), dimensions={1} | reverse | bytes 131072 | tf_op jit(solution)/shard_map/rev | solution.py:36
  215.4 1.4 slice.706
  216.9 1.3 slice.626
  218.2 1.5 slice.625
  239.1 1.6 pad.188
  240.7 1.8 pad.189
  242.6 20.6 %rev.13 = f32[2,8192]{1,0:T(2,128)} reverse(f32[2,8192]{1,0:T(2,128)S(1)} %add.446), dimensions={1} | reverse | bytes 131072 | tf_op jit(solution)/shard_map/rev | solution.py:82
  263.3 4.5 %all-to-all-start.2 = ((f32[2,16,512]{2,0,1:T(2,128)}), f32[2,16,512]{2,0,1:T(2,128)S(1)}, u32[]{:S(2)}, u32[]{:S(2)}) async-start(f32[2,16,512]{2,0,1:T(2,128)} %bitcast.21), calls=%async_computation.2 | async-start | bytes 131072 | tf_op jit(solution)/shard_map/all_to_all | solution.py:83
  267.9 5.9 %all-to-all-done.2 = f32[2,16,512]{2,0,1:T(2,128)S(1)} async-done(((f32[2,16,512]{2,0,1:T(2,128)}), f32[2,16,512]{2,0,1:T(2,128)S(1)}, u32[]{:S(2)}, u32[]{:S(2)}) %all-to-all-start.2) | async-done | bytes 65568 | tf_op jit(solution)/shard_map/all_to_all | solution.py:83
  275.5 4.8 %collective-permute-start.1 = (f32[8,16,1,512]{3,0,2,1:T(8,128)S(1)}, f32[8,16,1,512]{3,0,2,1:T(8,128)S(1)}, u32[]{:S(2)}, u32[]{:S(2)}) collective-permute-start(f32[8,16,1,512]{3,0,2,1:T(8,128)S(1)} %get-tuple-element.47), channel_id=1, source_target_pairs={{0,16},{16,32},{32,48},{48,64},{64,80},{80,96},{96,112},{112,128},... | collective-permute-start | bytes 786440 | tf_op jit(solution)/shard_map/ppermute | solution.py:23
  280.4 1.9 collective-permute-start
  282.3 1.4 collective-permute-done.1
  283.7 14.4 %collective-permute-done = f32[8,16,1,512]{3,0,2,1:T(8,128)S(1)} collective-permute-done((f32[8,16,1,512]{3,0,2,1:T(8,128)S(1)}, f32[8,16,1,512]{3,0,2,1:T(8,128)S(1)}, u32[]{:S(2)}, u32[]{:S(2)}) %collective-permute-start) | collective-permute-done | bytes 262176 | tf_op jit(solution)/shard_map/ppermute | solution.py:24
  298.0 0.9 pad_maximum_fusion.21
  298.9 5.1 %collective-permute-start.2 = (f32[8,16,6,1]{3,0,2,1:T(8,128)}, f32[8,16,6,1]{3,0,2,1:T(8,128)S(1)}, u32[]{:S(2)}, u32[]{:S(2)}) collective-permute-start(f32[8,16,6,1]{3,0,2,1:T(8,128)} %get-tuple-element.43), channel_id=1, source_target_pairs={{1,0},{2,1},{3,2},{4,3},{5,4},{6,5},{7,6},{8,7},{9,8},{10,9},{11,1... | collective-permute-start | bytes 9224 | tf_op jit(solution)/shard_map/ppermute | solution.py:24
  304.0 1.9 collective-permute-start.3
  306.0 6.9 %collective-permute-done.2 = f32[8,16,6,1]{3,0,2,1:T(8,128)S(1)} collective-permute-done((f32[8,16,6,1]{3,0,2,1:T(8,128)}, f32[8,16,6,1]{3,0,2,1:T(8,128)S(1)}, u32[]{:S(2)}, u32[]{:S(2)}) %collective-permute-start.2) | collective-permute-done | bytes 3104 | tf_op jit(solution)/shard_map/ppermute | solution.py:24
  313.7 4.3 collective-permute-done.3
  318.0 2.3 fusion.8
  320.7 11.0 %all_to_all.76 = f32[16,2,512]{2,1,0:T(2,128)S(1)} all-to-all(f32[16,2,512]{2,1,0:T(2,128)S(1)} %all_to_all.64), channel_id=1, replica_groups=mesh['wide'=32,'grp'=16] {'grp'}, dimensions={0} | all-to-all | bytes 131072 | tf_op jit(solution)/shard_map/all_to_all | solution.py:78
  331.6 5.6 %rev.14 = f32[2,8192]{1,0:T(2,128)S(1)} reverse(f32[2,8192]{1,0:T(2,128)S(1)} %bitcast.71), dimensions={1} | reverse | bytes 131072 | tf_op jit(solution)/shard_map/rev | solution.py:36
  337.3 1.4 slice.778
  338.8 1.3 slice.719
  340.1 1.3 slice.718
  366.7 1.6 pad.214
  368.3 1.9 pad.215
  370.3 5.6 %rev.15 = f32[2,8192]{1,0:T(2,128)S(1)} reverse(f32[2,8192]{1,0:T(2,128)S(1)} %add.491), dimensions={1} | reverse | bytes 131072 | tf_op jit(solution)/shard_map/rev | solution.py:82
  375.8 9.6 %all_to_all.77 = f32[2,16,512]{2,0,1:T(2,128)S(1)} all-to-all(f32[2,16,512]{2,0,1:T(2,128)S(1)} %bitcast.72), channel_id=1, replica_groups=mesh['wide'=32,'grp'=16] {'grp'}, dimensions={1} | all-to-all | bytes 131072 | tf_op jit(solution)/shard_map/all_to_all | solution.py:83
  387.1 8.9 %collective-permute-start.5 = (f32[8,16,1,512]{3,0,2,1:T(8,128)S(1)}, f32[8,16,1,512]{3,0,2,1:T(8,128)S(1)}, u32[]{:S(2)}, u32[]{:S(2)}) collective-permute-start(f32[8,16,1,512]{3,0,2,1:T(8,128)S(1)} %get-tuple-element.45), channel_id=1, source_target_pairs={{0,16},{16,32},{32,48},{48,64},{64,80},{80,96},{96,112},{112,128},... | collective-permute-start | bytes 786440 | tf_op jit(solution)/shard_map/ppermute | solution.py:23
  396.0 1.9 collective-permute-start.4
  397.9 10.6 %collective-permute-done.5 = f32[8,16,1,512]{3,0,2,1:T(8,128)S(1)} collective-permute-done((f32[8,16,1,512]{3,0,2,1:T(8,128)S(1)}, f32[8,16,1,512]{3,0,2,1:T(8,128)S(1)}, u32[]{:S(2)}, u32[]{:S(2)}) %collective-permute-start.5) | collective-permute-done | bytes 262176 | tf_op jit(solution)/shard_map/ppermute | solution.py:23
  408.5 2.8 collective-permute-done.4
  411.3 1.0 pad_maximum_fusion.18
  412.3 5.2 %collective-permute-start.6 = (f32[8,16,6,1]{3,0,2,1:T(8,128)}, f32[8,16,6,1]{3,0,2,1:T(8,128)}, u32[]{:S(2)}, u32[]{:S(2)}) collective-permute-start(f32[8,16,6,1]{3,0,2,1:T(8,128)} %get-tuple-element.41), channel_id=1, source_target_pairs={{1,0},{2,1},{3,2},{4,3},{5,4},{6,5},{7,6},{8,7},{9,8},{10,9},{11,1... | collective-permute-start | bytes 9224 | tf_op jit(solution)/shard_map/ppermute | solution.py:24
  417.5 1.9 collective-permute-start.7
  420.1 5.0 %collective-permute-done.6 = f32[8,16,6,1]{3,0,2,1:T(8,128)} collective-permute-done((f32[8,16,6,1]{3,0,2,1:T(8,128)}, f32[8,16,6,1]{3,0,2,1:T(8,128)}, u32[]{:S(2)}, u32[]{:S(2)}) %collective-permute-start.6) | collective-permute-done | bytes 3104 | tf_op jit(solution)/shard_map/ppermute | solution.py:24
  425.1 6.1 %collective-permute-done.7 = f32[8,16,6,1]{3,0,2,1:T(8,128)} collective-permute-done((f32[8,16,6,1]{3,0,2,1:T(8,128)}, f32[8,16,6,1]{3,0,2,1:T(8,128)}, u32[]{:S(2)}, u32[]{:S(2)}) %collective-permute-start.7) | collective-permute-done | bytes 3104 | tf_op jit(solution)/shard_map/ppermute | solution.py:23
  431.2 1.9 fusion.4
  433.2 1.6 copy.75
  (392 shorter events, 56.6 us)
Async XLA Ops:
  0.6 195.2 %copy-start = (f32[8,8]{1,0:T(8,128)S(1)}, f32[8,8]{1,0:T(8,128)}, u32[]{:S(2)}) copy-start(f32[8,8]{1,0:T(8,128)} %param.22) | copy-start | bytes 772
  1.9 170.1 %all-to-all-start = ((f32[32,1,128]{2,1,0:T(1,128)}), f32[32,1,128]{2,1,0:T(1,128)S(1)}, u32[]{:S(2)}, u32[]{:S(2)}) async-start(f32[32,1,128]{2,1,0:T(1,128)} %stack.2), calls=%async_computation | async-start | bytes 32768 | tf_op jit(solution)/shard_map/all_to_all | solution.py:12
  119.8 95.5 %copy-start.44 = (f32[2]{0:T(128)}, f32[2]{0:T(128)S(1)}, u32[]{:S(2)}) copy-start(f32[2]{0:T(128)S(1)} %get-tuple-element.65) | copy-start | bytes 28
  119.8 108.0 %copy-start.46 = (f32[2]{0:T(128)}, f32[2]{0:T(128)S(1)}, u32[]{:S(2)}) copy-start(f32[2]{0:T(128)S(1)} %get-tuple-element.37) | copy-start | bytes 28
  119.8 109.8 %copy-start.22 = (f32[2]{0:T(128)}, f32[2]{0:T(128)S(1)}, u32[]{:S(2)}) copy-start(f32[2]{0:T(128)S(1)} %get-tuple-element.38) | copy-start | bytes 28
  119.9 112.9 %copy-start.20 = (f32[2]{0:T(128)}, f32[2]{0:T(128)S(1)}, u32[]{:S(2)}) copy-start(f32[2]{0:T(128)S(1)} %get-tuple-element.39) | copy-start | bytes 28
  119.9 110.2 %copy-start.32 = (f32[2]{0:T(128)}, f32[2]{0:T(128)S(1)}, u32[]{:S(2)}) copy-start(f32[2]{0:T(128)S(1)} %get-tuple-element.68) | copy-start | bytes 28
  119.9 110.7 %copy-start.30 = (f32[2]{0:T(128)}, f32[2]{0:T(128)S(1)}, u32[]{:S(2)}) copy-start(f32[2]{0:T(128)S(1)} %get-tuple-element.66) | copy-start | bytes 28
  119.9 111.6 %copy-start.40 = (f32[2]{0:T(128)}, f32[2]{0:T(128)S(1)}, u32[]{:S(2)}) copy-start(f32[2]{0:T(128)S(1)} %get-tuple-element.67) | copy-start | bytes 28
  119.9 114.2 %copy-start.28 = (f32[2]{0:T(128)}, f32[2]{0:T(128)S(1)}, u32[]{:S(2)}) copy-start(f32[2]{0:T(128)S(1)} %get-tuple-element.61) | copy-start | bytes 28
  119.9 115.9 %copy-start.26 = (f32[2]{0:T(128)}, f32[2]{0:T(128)S(1)}, u32[]{:S(2)}) copy-start(f32[2]{0:T(128)S(1)} %get-tuple-element.62) | copy-start | bytes 28
  194.0 0.7 copy-start.52
  194.7 1.2 copy-start.14
  196.8 12.9 %all-to-all-start.1 = ((f32[16,2,512]{2,1,0:T(2,128)}), f32[16,2,512]{2,1,0:T(2,128)S(1)}, u32[]{:S(2)}, u32[]{:S(2)}) async-start(f32[16,2,512]{2,1,0:T(2,128)} %all_to_all.57), calls=%async_computation.1 | async-start | bytes 131072 | tf_op jit(solution)/shard_map/all_to_all | solution.py:78
  203.9 24.7 %copy-start.38 = (f32[2]{0:T(128)}, f32[2]{0:T(128)S(1)}, u32[]{:S(2)}) copy-start(f32[2]{0:T(128)S(1)} %get-tuple-element.57) | copy-start | bytes 28
  203.9 25.0 %copy-start.36 = (f32[2]{0:T(128)}, f32[2]{0:T(128)S(1)}, u32[]{:S(2)}) copy-start(f32[2]{0:T(128)S(1)} %get-tuple-element.63) | copy-start | bytes 28
  203.9 25.3 %copy-start.34 = (f32[2]{0:T(128)}, f32[2]{0:T(128)S(1)}, u32[]{:S(2)}) copy-start(f32[2]{0:T(128)S(1)} %get-tuple-element.58) | copy-start | bytes 28
  204.0 24.0 %copy-start.48 = (f32[2,1]{1,0:T(2,128)}, f32[2,1]{1,0:T(2,128)S(1)}, u32[]{:S(2)}) copy-start(f32[2,1]{1,0:T(2,128)S(1)} %copy.64) | copy-start | bytes 28
  204.7 23.5 %copy-start.50 = (f32[2,1]{1,0:T(2,128)}, f32[2,1]{1,0:T(2,128)S(1)}, u32[]{:S(2)}) copy-start(f32[2,1]{1,0:T(2,128)S(1)} %copy.65) | copy-start | bytes 28
  204.9 69.1 %copy-start.24 = (f32[8]{0:T(128)}, f32[8]{0:T(128)S(1)}, u32[]{:S(2)}) copy-start(f32[8]{0:T(128)S(1)} %select_reduce_fusion) | copy-start | bytes 100
  215.4 2.8 copy-start.5
  219.8 1.3 copy-start.7
  221.8 0.7 copy-start.9
  231.6 0.7 slice-start.8
  238.3 0.7 slice-start.1
  263.3 10.5 %all-to-all-start.2 = ((f32[2,16,512]{2,0,1:T(2,128)}), f32[2,16,512]{2,0,1:T(2,128)S(1)}, u32[]{:S(2)}, u32[]{:S(2)}) async-start(f32[2,16,512]{2,0,1:T(2,128)} %bitcast.21), calls=%async_computation.2 | async-start | bytes 131072 | tf_op jit(solution)/shard_map/all_to_all | solution.py:83
  267.7 6.2 %copy-start.42 = (f32[8]{0:T(128)}, f32[8]{0:T(128)S(1)}, u32[]{:S(2)}) copy-start(f32[8]{0:T(128)S(1)} %broadcast_subtract_fusion) | copy-start | bytes 100
  273.9 0.7 copy-start.13
  274.6 0.9 copy-start.1
  275.5 8.1 %collective-permute-start.1 = (f32[8,16,1,512]{3,0,2,1:T(8,128)S(1)}, f32[8,16,1,512]{3,0,2,1:T(8,128)S(1)}, u32[]{:S(2)}, u32[]{:S(2)}) collective-permute-start(f32[8,16,1,512]{3,0,2,1:T(8,128)S(1)} %get-tuple-element.47), channel_id=1, source_target_pairs={{0,16},{16,32},{32,48},{48,64},{64,80},{80,96},{96,112},{112,128},... | collective-permute-start | bytes 786440 | tf_op jit(solution)/shard_map/ppermute | solution.py:23
  280.4 17.7 %collective-permute-start = (f32[8,16,1,512]{3,0,2,1:T(8,128)S(1)}, f32[8,16,1,512]{3,0,2,1:T(8,128)S(1)}, u32[]{:S(2)}, u32[]{:S(2)}) collective-permute-start(f32[8,16,1,512]{3,0,2,1:T(8,128)S(1)} %get-tuple-element.48), channel_id=1, source_target_pairs={{16,0},{32,16},{48,32},{64,48},{80,64},{96,80},{112,96},{128,112},... | collective-permute-start | bytes 786440 | tf_op jit(solution)/shard_map/ppermute | solution.py:24
  298.0 0.9 copy-start.3
  298.9 14.0 %collective-permute-start.2 = (f32[8,16,6,1]{3,0,2,1:T(8,128)}, f32[8,16,6,1]{3,0,2,1:T(8,128)S(1)}, u32[]{:S(2)}, u32[]{:S(2)}) collective-permute-start(f32[8,16,6,1]{3,0,2,1:T(8,128)} %get-tuple-element.43), channel_id=1, source_target_pairs={{1,0},{2,1},{3,2},{4,3},{5,4},{6,5},{7,6},{8,7},{9,8},{10,9},{11,1... | collective-permute-start | bytes 9224 | tf_op jit(solution)/shard_map/ppermute | solution.py:24
  304.0 14.0 %collective-permute-start.3 = (f32[8,16,6,1]{3,0,2,1:T(8,128)S(1)}, f32[8,16,6,1]{3,0,2,1:T(8,128)}, u32[]{:S(2)}, u32[]{:S(2)}) collective-permute-start(f32[8,16,6,1]{3,0,2,1:T(8,128)S(1)} %get-tuple-element.44), channel_id=1, source_target_pairs={{0,1},{1,2},{2,3},{3,4},{4,5},{5,6},{6,7},{7,8},{8,9},{9,10},{10,1... | collective-permute-start | bytes 9224 | tf_op jit(solution)/shard_map/ppermute | solution.py:23
  306.0 14.3 %copy-start.15 = (f32[4,512]{1,0:T(4,128)S(1)}, f32[4,512]{1,0:T(4,128)}, u32[]{:S(2)}) copy-start(f32[4,512]{1,0:T(4,128)} %param.21) | copy-start | bytes 24580
  312.9 0.8 copy-start.6
  331.6 5.6 %copy-start.45 = (f32[2]{0:T(128)S(1)}, f32[2]{0:T(128)}, u32[]{:S(2)}) copy-start(f32[2]{0:T(128)} %copy-done.44) | copy-start | bytes 28
  337.3 2.8 copy-start.4
  341.5 1.3 copy-start.8
  343.5 0.7 copy-start.10
  348.2 0.7 copy-start.31
  359.2 0.7 slice-start.9
  363.4 0.7 slice-start.3
  387.1 21.4 %collective-permute-start.5 = (f32[8,16,1,512]{3,0,2,1:T(8,128)S(1)}, f32[8,16,1,512]{3,0,2,1:T(8,128)S(1)}, u32[]{:S(2)}, u32[]{:S(2)}) collective-permute-start(f32[8,16,1,512]{3,0,2,1:T(8,128)S(1)} %get-tuple-element.45), channel_id=1, source_target_pairs={{0,16},{16,32},{32,48},{48,64},{64,80},{80,96},{96,112},{112,128},... | collective-permute-start | bytes 786440 | tf_op jit(solution)/shard_map/ppermute | solution.py:23
  396.0 15.3 %collective-permute-start.4 = (f32[8,16,1,512]{3,0,2,1:T(8,128)S(1)}, f32[8,16,1,512]{3,0,2,1:T(8,128)S(1)}, u32[]{:S(2)}, u32[]{:S(2)}) collective-permute-start(f32[8,16,1,512]{3,0,2,1:T(8,128)S(1)} %get-tuple-element.46), channel_id=1, source_target_pairs={{16,0},{32,16},{48,32},{64,48},{80,64},{96,80},{112,96},{128,112},... | collective-permute-start | bytes 786440 | tf_op jit(solution)/shard_map/ppermute | solution.py:24
  411.3 1.0 copy-start.2
  412.3 12.8 %collective-permute-start.6 = (f32[8,16,6,1]{3,0,2,1:T(8,128)}, f32[8,16,6,1]{3,0,2,1:T(8,128)}, u32[]{:S(2)}, u32[]{:S(2)}) collective-permute-start(f32[8,16,6,1]{3,0,2,1:T(8,128)} %get-tuple-element.41), channel_id=1, source_target_pairs={{1,0},{2,1},{3,2},{4,3},{5,4},{6,5},{7,6},{8,7},{9,8},{10,9},{11,1... | collective-permute-start | bytes 9224 | tf_op jit(solution)/shard_map/ppermute | solution.py:24
  417.5 13.8 %collective-permute-start.7 = (f32[8,16,6,1]{3,0,2,1:T(8,128)}, f32[8,16,6,1]{3,0,2,1:T(8,128)}, u32[]{:S(2)}, u32[]{:S(2)}) collective-permute-start(f32[8,16,6,1]{3,0,2,1:T(8,128)} %get-tuple-element.42), channel_id=1, source_target_pairs={{0,1},{1,2},{2,3},{3,4},{4,5},{5,6},{6,7},{7,8},{8,9},{9,10},{10,1... | collective-permute-start | bytes 9224 | tf_op jit(solution)/shard_map/ppermute | solution.py:23
  (36 other events, 23.3 us)
